TPU v7x, 32 devices: a whole 2x2x4 slice. The times are simulated.
32 devices in a mesh: row: 4 (over y, x), col: 8 (over z, core).
Axes of the slice: x: 2, y: 2, z: 4, core: 2. Of those that a mesh axis runs over, the one named last changes fastest.
Arguments:
- block_input: float32 [2, 8192, 640], P(None, ('row', 'col')), may hold values from -6 to 6
- output_grad: float32 [2, 8192, 640], P(None, ('row', 'col')), may hold values from -6 to 6
- sequence_ids: int32 [2, 8192], P(None, ('row', 'col')), may hold values from 0 to 7, as said below
- attn_weights: float32 [640, 2560], P(None, ('row', 'col')), may hold values from -0.29646353 to 0.29646353
- attn_momentum: float32 [640, 2560], P(None, ('row', 'col')), may hold values from -422.4 to 422.4
- attn_average: float32 [640, 2560], P(None, ('row', 'col')), may hold values from -0.29646353 to 0.29646353
- norm_params: float32 [2560], P(('row', 'col')), may hold values from -0.6 to 1.3
- norm_momentum: float32 [2560], P(('row', 'col')), may hold values from -806.4 to 806.4
- norm_average: float32 [2560], P(('row', 'col')), may hold values from -0.6 to 1.3
- ffn_weights: float32 [2, 640, 5120], P(None, 'row', 'col'), may hold values from -0.118585412 to 0.118585412
- ffn_momentum: float32 [2, 640, 5120], P(None, 'row', 'col'), may hold values from -249.6 to 249.6
- ffn_average: float32 [2, 640, 5120], P(None, 'row', 'col'), may hold values from -0.118585412 to 0.118585412
Outputs:
- block_output: float32 [2, 8192, 640], P(None, ('row', 'col'))
- input_grad: float32 [2, 8192, 640], P(None, ('row', 'col'))
- attn_grad: float32 [640, 2560], P(None, ('row', 'col'))
- attn_momentum_new: float32 [640, 2560], P(None, ('row', 'col'))
- attn_weights_new: float32 [640, 2560], P(None, ('row', 'col'))
- attn_average_new: float32 [640, 2560], P(None, ('row', 'col'))
- attn_copy: bfloat16 [640, 2560], P(None, ('row', 'col'))
- norm_grad: float32 [2560], P(('row', 'col'))
- norm_momentum_new: float32 [2560], P(('row', 'col'))
- norm_params_new: float32 [2560], P(('row', 'col'))
- norm_average_new: float32 [2560], P(('row', 'col'))
- norm_copy: bfloat16 [2560], P(('row', 'col'))
- ffn_grad: float32 [2, 640, 5120], P(None, 'row', 'col')
- ffn_momentum_new: float32 [2, 640, 5120], P(None, 'row', 'col')
- ffn_weights_new: float32 [2, 640, 5120], P(None, 'row', 'col')
- ffn_average_new: float32 [2, 640, 5120], P(None, 'row', 'col')
- ffn_copy: bfloat16 [2, 640, 5120], P(None, 'row', 'col')
Inputs may be any that keep to these rules, and one draw needn't show every extreme that they name: `sequence_ids`: within each aligned block of 256 tokens the numbers start at 0, never fall and step by one; a sequence (a run of equal numbers) holds 20 to 256 tokens; in each micro-batch one block holds a single sequence and another holds 8 sequences.
All inputs are finite; a program needn't handle non-finite values.
Results may differ from a plain program's by a relative error of at most 0.014.
The roundings to bfloat16 on the way count: a program that leaves them out, or rounds other values in their place, can miss the bound.
Values may be sent and summed in bfloat16 or wider, within the bound.
A program may use at most 128 MiB of HBM per device.

v0:
```python
import math
import jax
import jax.numpy as jnp
from jax import lax
from jax.sharding import PartitionSpec as P

D = 640
H = 20
HD = 32
MB = 2
EPSILON = 1e-05
MOMENT_DECAY = 0.9
AVERAGE_DECAY = 0.85
RATE_SCALE = 0.06
MASKED = -1e30


def layer_norm(values, gain, shift):
    center = values - jnp.mean(values, axis=-1, keepdims=True)
    spread = jnp.mean(center * center, axis=-1, keepdims=True)
    return center * lax.rsqrt(spread + EPSILON) * gain + shift


def gelu_exact(values):
    return jax.nn.gelu(values, approximate=False)


def matmul(left_side, right_side):
    return jnp.dot(left_side, right_side, preferred_element_type=jnp.float32)


def contract_rows(left_side, right_side):
    return lax.dot_general(
        left_side, right_side, (((0,), (0,)), ((), ())), preferred_element_type=jnp.float32
    )


def contract_cols(left_side, right_side):
    return lax.dot_general(
        left_side, right_side, (((1,), (1,)), ((), ())), preferred_element_type=jnp.float32
    )


def head_slices(qkv_low, first_col, head_group):
    length = qkv_low.shape[0]
    group_width = head_group * HD
    queries = lax.dynamic_slice_in_dim(qkv_low, first_col, group_width, 1).reshape(
        length, head_group, HD
    )
    keys_part = lax.dynamic_slice_in_dim(qkv_low, D + first_col, group_width, 1).reshape(
        length, head_group, HD
    )
    values = lax.dynamic_slice_in_dim(qkv_low, 2 * D + first_col, group_width, 1).reshape(
        length, head_group, HD
    )
    return (queries, keys_part, values)


def masked_scores(queries, keys_part, same_seq):
    scores = jnp.einsum(
        "qhe,khe->hqk", queries, keys_part, preferred_element_type=jnp.float32
    ) * HD ** (-0.5)
    return jnp.where(same_seq[None], scores, MASKED)


def attend_forward(qkv_low, same_seq):
    length = qkv_low.shape[0]
    head_group = math.gcd(H, 4)
    group_width = head_group * HD

    def one_group(group_index, state_all):
        mixed_all, maxima, totals = state_all
        first_col = group_index * group_width
        queries, keys_part, values = head_slices(qkv_low, first_col, head_group)
        scores = masked_scores(queries, keys_part, same_seq)
        row_max = jnp.max(scores, axis=-1, keepdims=True)
        exponent = jnp.exp(scores - row_max)
        row_total = jnp.sum(exponent, axis=-1, keepdims=True)
        attn_probs = (exponent / row_total).astype(jnp.bfloat16)
        mixed_rows = jnp.einsum(
            "hqk,khe->qhe", attn_probs, values, preferred_element_type=jnp.float32
        )
        mixed_all = lax.dynamic_update_slice_in_dim(
            mixed_all, mixed_rows.reshape(length, group_width), first_col, 1
        )
        maxima = lax.dynamic_update_slice_in_dim(
            maxima, row_max[:, :, 0], group_index * head_group, 0
        )
        totals = lax.dynamic_update_slice_in_dim(
            totals, row_total[:, :, 0], group_index * head_group, 0
        )
        return (mixed_all, maxima, totals)

    initial = (
        jnp.zeros((length, D), jnp.float32),
        jnp.zeros((H, length), jnp.float32),
        jnp.zeros((H, length), jnp.float32),
    )
    return lax.fori_loop(0, H // head_group, one_group, initial)


def attend_backward(qkv_low, same_seq, maxima, totals, grad_mixed):
    length = qkv_low.shape[0]
    head_group = math.gcd(H, 4)
    group_width = head_group * HD

    def one_group(group_index, grad_qkv):
        first_col = group_index * group_width
        queries, keys_part, values = head_slices(qkv_low, first_col, head_group)
        grad_part = lax.dynamic_slice_in_dim(grad_mixed, first_col, group_width, 1).reshape(
            length, head_group, HD
        )
        scores = masked_scores(queries, keys_part, same_seq)
        row_max = lax.dynamic_slice_in_dim(maxima, group_index * head_group, head_group, 0)[
            :, :, None
        ]
        row_total = lax.dynamic_slice_in_dim(totals, group_index * head_group, head_group, 0)[
            :, :, None
        ]
        attn_probs = jnp.exp(scores - row_max) / row_total
        grad_probs = jnp.einsum(
            "qhe,khe->hqk", grad_part, values, preferred_element_type=jnp.float32
        )
        grad_values = jnp.einsum(
            "hqk,qhe->khe",
            attn_probs.astype(jnp.bfloat16),
            grad_part,
            preferred_element_type=jnp.float32,
        )
        grad_scores = attn_probs * (
            grad_probs - jnp.sum(grad_probs * attn_probs, axis=-1, keepdims=True)
        )
        grad_scores = grad_scores.astype(jnp.bfloat16)
        grad_queries = jnp.einsum(
            "hqk,khe->qhe", grad_scores, keys_part, preferred_element_type=jnp.float32
        ) * HD ** (-0.5)
        grad_keys = jnp.einsum(
            "hqk,qhe->khe", grad_scores, queries, preferred_element_type=jnp.float32
        ) * HD ** (-0.5)
        for offset, grad_piece in ((0, grad_queries), (D, grad_keys), (2 * D, grad_values)):
            grad_qkv = lax.dynamic_update_slice_in_dim(
                grad_qkv, grad_piece.reshape(length, group_width), offset + first_col, 1
            )
        return grad_qkv

    return lax.fori_loop(0, H // head_group, one_group, jnp.zeros((length, 3 * D), jnp.float32))


def sgd_update(weights_old, moment, average, grad_sum, step_rate):
    moment_new = MOMENT_DECAY * moment + grad_sum
    weights_new = weights_old - step_rate * (grad_sum + MOMENT_DECAY * moment_new)
    average_new = AVERAGE_DECAY * average + (1.0 - AVERAGE_DECAY) * weights_new
    return (moment_new, weights_new, average_new, weights_new.astype(jnp.bfloat16))


def local(
    block_input,
    output_grad,
    sequence_ids,
    attn_weights,
    attn_momentum,
    attn_average,
    norm_params,
    norm_momentum,
    norm_average,
    ffn_weights,
    ffn_momentum,
    ffn_average,
):
    attn_full, norm_full = (
        lax.all_gather(attn_weights.astype(jnp.bfloat16), ("row", "col"), axis=1, tiled=True),
        lax.all_gather(norm_params.astype(jnp.bfloat16), ("row", "col"), axis=0, tiled=True),
    )
    norm_values = norm_full.astype(jnp.float32)
    gain_one = norm_values[:D]
    shift_one = norm_values[D : 2 * D]
    gain_two = norm_values[2 * D : 3 * D]
    shift_two = norm_values[3 * D :]
    qkv_weights = attn_full[:, : 3 * D]
    out_weights = attn_full[:, 3 * D :]
    ffn_rows = lax.all_gather(ffn_weights.astype(jnp.bfloat16), "row", axis=1, tiled=True)
    col_width = ffn_weights.shape[2]
    length = block_input.shape[1]
    attn_acc = jnp.zeros((D, 4 * D), jnp.float32)
    norm_acc = jnp.zeros((4 * D,), jnp.float32)
    ffn_acc = jnp.zeros((2, D, col_width), jnp.float32)
    outputs_all = []
    grads_all = []
    for micro_step in range(MB):
        inputs = block_input[micro_step]
        ids_row = sequence_ids[micro_step]
        same_seq = ids_row[:, None] == ids_row[None, :]
        normed, pull_one = jax.vjp(layer_norm, inputs, gain_one, shift_one)
        normed_low = normed.astype(jnp.bfloat16)
        qkv_low = matmul(normed_low, qkv_weights).astype(jnp.bfloat16)
        mixed_all, maxima, totals = attend_forward(qkv_low, same_seq)
        mixed_low = mixed_all.astype(jnp.bfloat16)
        hidden_in = inputs + matmul(mixed_low, out_weights)
        normed_two, pull_two = jax.vjp(layer_norm, hidden_in, gain_two, shift_two)
        normed_two_low = normed_two.astype(jnp.bfloat16)
        grad_out = output_grad[micro_step]
        grad_out_low = grad_out.astype(jnp.bfloat16)
        normed_all = lax.all_gather(normed_two_low, "col", axis=0, tiled=True)
        up_proj = matmul(normed_all, ffn_rows[0])
        activation, pull_gelu = jax.vjp(gelu_exact, up_proj)
        activ_low = activation.astype(jnp.bfloat16)
        ffn_out = lax.psum_scatter(
            contract_cols(activ_low, ffn_rows[1]).astype(jnp.bfloat16),
            "col",
            scatter_dimension=0,
            tiled=True,
        ).astype(jnp.float32)
        grad_all = lax.all_gather(grad_out_low, "col", axis=0, tiled=True)
        grad_act = matmul(grad_all, ffn_rows[1])
        grad_up = pull_gelu(grad_act)[0].astype(jnp.bfloat16)
        grad_normed_two = lax.psum_scatter(
            contract_cols(grad_up, ffn_rows[0]).astype(jnp.bfloat16),
            "col",
            scatter_dimension=0,
            tiled=True,
        ).astype(jnp.float32)
        ffn_acc = ffn_acc + jnp.stack(
            [contract_rows(normed_all, grad_up), contract_rows(grad_all, activ_low)]
        )
        outputs_all.append(hidden_in + ffn_out)
        grad_ln_two, gain_two_grad, shift_two_grad = pull_two(grad_normed_two)
        grad_hidden = grad_out + grad_ln_two
        grad_branch_low = grad_hidden.astype(jnp.bfloat16)
        out_proj_grad = contract_rows(mixed_low, grad_branch_low)
        grad_mixed_low = contract_cols(grad_branch_low, out_weights).astype(jnp.bfloat16)
        grad_qkv_low = attend_backward(qkv_low, same_seq, maxima, totals, grad_mixed_low).astype(
            jnp.bfloat16
        )
        qkv_grad = contract_rows(normed_low, grad_qkv_low)
        grad_normed = contract_cols(grad_qkv_low, qkv_weights)
        grad_ln_one, gain_one_grad, shift_one_grad = pull_one(grad_normed)
        grads_all.append(grad_hidden + grad_ln_one)
        attn_acc = attn_acc + jnp.concatenate([qkv_grad, out_proj_grad], axis=1)
        norm_acc = norm_acc + jnp.concatenate(
            [gain_one_grad, shift_one_grad, gain_two_grad, shift_two_grad]
        )
    ffn_grad = lax.psum_scatter(
        ffn_acc.astype(jnp.bfloat16), "row", scatter_dimension=1, tiled=True
    ).astype(jnp.float32)
    attn_grad, norm_grad = (
        lax.psum_scatter(attn_acc, ("row", "col"), scatter_dimension=1, tiled=True),
        lax.psum_scatter(norm_acc, ("row", "col"), scatter_dimension=0, tiled=True),
    )
    total_tokens = MB * length * lax.axis_size("row") * lax.axis_size("col")
    step_rate = RATE_SCALE * total_tokens ** (-0.5)
    attn_moment_new, attn_new, attn_avg_new, attn_copy = sgd_update(
        attn_weights, attn_momentum, attn_average, attn_grad, step_rate
    )
    norm_moment_new, norm_new, norm_avg_new, norm_copy = sgd_update(
        norm_params, norm_momentum, norm_average, norm_grad, step_rate
    )
    ffn_moment_new, ffn_new, ffn_avg_new, ffn_copy = sgd_update(
        ffn_weights, ffn_momentum, ffn_average, ffn_grad, step_rate
    )
    return (
        jnp.stack(outputs_all),
        jnp.stack(grads_all),
        attn_grad,
        attn_moment_new,
        attn_new,
        attn_avg_new,
        attn_copy,
        norm_grad,
        norm_moment_new,
        norm_new,
        norm_avg_new,
        norm_copy,
        ffn_grad,
        ffn_moment_new,
        ffn_new,
        ffn_avg_new,
        ffn_copy,
    )


def solution(mesh):
    return jax.shard_map(
        local,
        mesh=mesh,
        in_specs=(
            P(None, ("row", "col"), None),
            P(None, ("row", "col"), None),
            P(None, ("row", "col")),
            P(None, ("row", "col")),
            P(None, ("row", "col")),
            P(None, ("row", "col")),
            P(("row", "col")),
            P(("row", "col")),
            P(("row", "col")),
            P(None, "row", "col"),
            P(None, "row", "col"),
            P(None, "row", "col"),
        ),
        out_specs=(
            P(None, ("row", "col"), None),
            P(None, ("row", "col"), None),
            P(None, ("row", "col")),
            P(None, ("row", "col")),
            P(None, ("row", "col")),
            P(None, ("row", "col")),
            P(None, ("row", "col")),
            P(("row", "col")),
            P(("row", "col")),
            P(("row", "col")),
            P(("row", "col")),
            P(("row", "col")),
            P(None, "row", "col"),
            P(None, "row", "col"),
            P(None, "row", "col"),
            P(None, "row", "col"),
            P(None, "row", "col"),
        ),
        check_vma=False,
    )
```

profile of v0, /device:TPU:0, one launch (start us, length us, event | category | flops | bytes accessed | tf_op | source)
XLA Modules:
  0.0 634.6 jit_solution(1245583940344998893)
XLA Ops:
  16.0 42.1 %all-reduce = bf16[2560]{0:T(1024)(128)(2,1)S(1)} all-reduce(bf16[2560]{0:T(1024)(128)(2,1)S(1)} %dynamic-update-slice), channel_id=1, replica_groups=mesh['row'=4,'col'=8] {'row','col'}, use_global_device_ids=true, to_apply=%add | all-reduce | flops 2560 | bytes 10240
  58.1 15.5 %all-gather.7.cloned.1.call-done = bf16[640,2560]{0,1:T(8,128)(2,1)} async-done(((bf16[640,80]{0,1:T(8,128)(2,1)}), bf16[640,2560]{0,1:T(8,128)(2,1)}) %all-gather.7.cloned.1.call-update) | async-done | bytes 3276816 | tf_op jit(solution)/shard_map/all_gather | solution.py:171
  73.6 3.0 convolution_convert_fusion.4
  77.3 5.3 while.73
  85.1 4.0 convolution_convert_fusion.5
  91.5 8.2 %while.72 = (s32[]{:T(128)}, bf16[256,640]{0,1:T(8,128)(2,1)}, f32[20,256]{1,0:T(8,128)S(1)}, f32[20,256]{1,0:T(8,128)S(1)}, bf16[256,1920]{0,1:T(8,128)(2,1)S(1...) while((s32[]{:T(128)}, bf16[256,640]{0,1:T(8,128)(2,1)}, ...), condition=%wide.region_5.6_spmd.clone, body=%wide.region_2.5_spmd.clone.sunk | while | flops 35715084 | bytes 4101494 | solution.py:99
  109.0 33.7 %all-gather.9.cloned.1.call-done = bf16[2048,640]{1,0:T(8,128)(2,1)} async-done(((bf16[256,640]{1,0:T(8,128)(2,1)}), bf16[2048,640]{1,0:T(8,128)(2,1)}) %all-gather.9.cloned.1.call-update) | async-done | bytes 2621456 | tf_op jit(solution)/shard_map/all_gather | solution.py:203
  142.7 16.6 %multiply_convert_fusion.3 = (bf16[2048,640]{1,0:T(8,128)(2,1)}, f32[2048,640]{1,0:T(8,128)}, f32[2048,640]{1,0:T(8,128)}) fusion(bf16[2048,640]{1,0:T(8,128)(2,1)} %all-gather.9.cloned.1.call-done, bf16[2,640,640]{2,1,0:T(8,128)(2,1)} %all-gather.11.cloned.1.call-done), kind=kOutput, calls=%fused_computation.92 | convolution fusion | flops 1762918400 | bytes 16547840 | tf_op jit(solution)/shard_map/dot_general | solution.py:29
  159.3 17.8 %all-gather.15.cloned.1.call-done = bf16[2048,640]{1,0:T(8,128)(2,1)} async-done(((bf16[256,640]{1,0:T(8,128)(2,1)}), bf16[2048,640]{1,0:T(8,128)(2,1)}) %all-gather.15.cloned.1.call-update) | async-done | bytes 2621456 | tf_op jit(solution)/shard_map/all_gather | solution.py:213
  177.1 8.6 %add_convert_fusion.1 = bf16[2048,640]{1,0:T(8,128)(2,1)S(1)} fusion(f32[2048,640]{1,0:T(8,128)} %get-tuple-element.929, f32[2048,640]{1,0:T(8,128)} %get-tuple-element.981, bf16[2048,640]{1,0:T(8,128)(2,1)} %all-gather.15.cloned.1.call-done, bf16[2,640,640]{2,1,0:T(8,128)(2,1)} %all-gather.11.cloned.1.call-done), kind=kOutput, calls=%fused_computation.78 | convolution fusion | flops 1696071680 | bytes 16547840 | tf_op jit(solution)/shard_map/dot_general | solution.py:29
  187.1 3.8 convolution_convert_fusion.1
  191.2 20.9 %all-gather.13.cloned.1.call-done = bf16[2048,640]{1,0:T(8,128)(2,1)} async-done(((bf16[256,640]{1,0:T(8,128)(2,1)}), bf16[2048,640]{1,0:T(8,128)(2,1)}) %all-gather.13.cloned.1.call-update) | async-done | bytes 2621456 | tf_op jit(solution)/shard_map/all_gather | solution.py:203
  212.0 16.5 %multiply_convert_fusion.2 = (bf16[2048,640]{1,0:T(8,128)(2,1)}, f32[2048,640]{1,0:T(8,128)}, f32[2048,640]{1,0:T(8,128)}) fusion(bf16[2048,640]{1,0:T(8,128)(2,1)} %all-gather.13.cloned.1.call-done, bf16[2,640,640]{2,1,0:T(8,128)(2,1)} %all-gather.11.cloned.1.call-done), kind=kOutput, calls=%fused_computation.79 | convolution fusion | flops 1762918400 | bytes 16547840 | tf_op jit(solution)/shard_map/dot_general | solution.py:29
  228.6 17.9 %all-gather.17.cloned.1.call-done = bf16[2048,640]{1,0:T(8,128)(2,1)} async-done(((bf16[256,640]{1,0:T(8,128)(2,1)}), bf16[2048,640]{1,0:T(8,128)(2,1)}) %all-gather.17.cloned.1.call-update) | async-done | bytes 2621456 | tf_op jit(solution)/shard_map/all_gather | solution.py:213
  246.4 8.6 %add_convert_fusion = bf16[2048,640]{1,0:T(8,128)(2,1)S(1)} fusion(f32[2048,640]{1,0:T(8,128)} %get-tuple-element.931, f32[2048,640]{1,0:T(8,128)} %get-tuple-element.982, bf16[2048,640]{1,0:T(8,128)(2,1)} %all-gather.17.cloned.1.call-done, bf16[2,640,640]{2,1,0:T(8,128)(2,1)} %all-gather.11.cloned.1.call-done), kind=kOutput, calls=%fused_computation.77 | convolution fusion | flops 1696071680 | bytes 16547840 | tf_op jit(solution)/shard_map/dot_general | solution.py:29
  256.6 3.7 convolution_convert_fusion
  260.4 6.0 convolution_convert_fusion.2
  266.8 5.9 convolution_convert_fusion.3
  272.9 5.0 convolution_bitcast_fusion
  288.3 35.8 %reduce-scatter.15.cloned.1.call-done = bf16[256,640]{1,0:T(8,128)(2,1)} async-done(((bf16[2048,640]{1,0:T(8,128)(2,1)}), bf16[256,640]{1,0:T(8,128)(2,1)}) %reduce-scatter.15.cloned.1.call-update) | async-done | bytes 327696 | tf_op jit(solution)/shard_map/reduce_scatter | solution.py:216
  327.1 36.2 %reduce-scatter.11.cloned.1.call-done = bf16[256,640]{1,0:T(8,128)(2,1)} async-done(((bf16[2048,640]{1,0:T(8,128)(2,1)}), bf16[256,640]{1,0:T(8,128)(2,1)}) %reduce-scatter.11.cloned.1.call-update) | async-done | bytes 327696 | tf_op jit(solution)/shard_map/reduce_scatter | solution.py:207
  363.3 38.9 %reduce-scatter.9.cloned.1.call-done = bf16[256,640]{1,0:T(8,128)(2,1)} async-done(((bf16[2048,640]{1,0:T(8,128)(2,1)}), bf16[256,640]{1,0:T(8,128)(2,1)}) %reduce-scatter.9.cloned.1.call-update) | async-done | bytes 327696 | tf_op jit(solution)/shard_map/reduce_scatter | solution.py:207
  402.1 2.8 bitcast_add_fusion.1
  407.4 15.2 %while.74 = (s32[]{:T(128)}, bf16[256,1920]{0,1:T(8,128)(2,1)S(1)}, bf16[256,1920]{0,1:T(8,128)(2,1)}, f32[20,256]{1,0:T(8,128)S(1)}, f32[20,256]{1,0:T(8,128)S(...) while((s32[]{:T(128)}, bf16[256,1920]{0,1:T(8,128)(2,1)S(1)}, ...), condition=%wide.region_23.24_spmd.clone, body=%wide.region_21.0_spmd.clone.sunk | while | flops 86703120 | bytes 9733514 | solution.py:146
  422.6 2.7 convolution_convert_fusion.6
  426.4 31.9 %while.75 = (s32[]{:T(128)}, bf16[256,1920]{0,1:T(8,128)(2,1)}, bf16[256,1920]{0,1:T(8,128)(2,1)}, f32[20,256]{1,0:T(8,128)}, f32[20,256]{1,0:T(8,128)}, /*index...) while((s32[]{:T(128)}, bf16[256,1920]{0,1:T(8,128)(2,1)}, ...), condition=%wide.region_31.32_spmd.clone, body=%wide.region_29.0_spmd.clone.sunk | while | flops 86703120 | bytes 9733514 | solution.py:146
  463.6 3.2 maximum_add_fusion
  466.9 8.2 %copy.93 = f32[640,2560]{0,1:T(8,128)} copy(f32[640,2560]{1,0:T(8,128)} %maximum_add_fusion) | data formatting | bytes 13107200
  478.7 3.2 fusion.83
  481.9 2.5 multiply_add_fusion
  488.8 39.0 %all-reduce.1 = f32[2560]{0:T(1024)S(1)} all-reduce(f32[2560]{0:T(1024)S(1)} %maximum_add_fusion.2), channel_id=7, replica_groups=mesh['row'=4,'col'=8] {'row','col'}, use_global_device_ids=true, to_apply=%region_43.44.clone | all-reduce | flops 2560 | bytes 20480
  534.5 87.4 %reduce-scatter.19.cloned.1.call-done = f32[80,640]{1,0:T(8,128)} async-done(((f32[2560,640]{1,0:T(8,128)}), f32[80,640]{1,0:T(8,128)}) %reduce-scatter.19.cloned.1.call-update) | async-done | bytes 204816
  (419 shorter events, 128.6 us)
Async XLA Ops:
  7.2 66.4 %all-gather.7.cloned.1.call-start = ((), (), s32[]{:S(2)}) async-start(), calls=%async_computation.6 | async-start | bytes 3379200 | tf_op jit(solution)/shard_map/all_gather | solution.py:171
  8.8 100.2 %all-gather.11.cloned.1.call-start = ((), (), s32[]{:S(2)}) async-start(), calls=%async_computation.8 | async-start | bytes 2048000 | tf_op jit(solution)/shard_map/all_gather | solution.py:181
  10.9 131.8 %all-gather.9.cloned.1.call-start = ((), (), s32[]{:S(2)}) async-start(), calls=%async_computation.7 | async-start | bytes 2949120 | tf_op jit(solution)/shard_map/all_gather | solution.py:203
  13.8 63.5 %copy-start.35 = (f32[256]{0:T(256)}, f32[256]{0:T(256)S(1)}, u32[]{:S(2)}) copy-start(f32[256]{0:T(256)S(1)} %get-tuple-element.984) | copy-start | bytes 3076
  13.8 68.8 %copy-start.37 = (f32[256]{0:T(256)}, f32[256]{0:T(256)S(1)}, u32[]{:S(2)}) copy-start(f32[256]{0:T(256)S(1)} %get-tuple-element.985) | copy-start | bytes 3076
  15.4 67.2 %copy-start.39 = (f32[256]{0:T(256)}, f32[256]{0:T(256)S(1)}, u32[]{:S(2)}) copy-start(f32[256]{0:T(256)S(1)} %fusion.77) | copy-start | bytes 3076
  15.4 61.8 %copy-start.41 = (f32[256]{0:T(256)}, f32[256]{0:T(256)S(1)}, u32[]{:S(2)}) copy-start(f32[256]{0:T(256)S(1)} %fusion.79) | copy-start | bytes 3076
  58.0 24.6 %copy-start.27 = (f32[640]{0:T(1024)}, f32[640]{0:T(1024)S(1)}, u32[]{:S(2)}) copy-start(f32[640]{0:T(1024)S(1)} %get-tuple-element.973) | copy-start | bytes 7684
  58.0 24.6 %copy-start.29 = (f32[640]{0:T(1024)}, f32[640]{0:T(1024)S(1)}, u32[]{:S(2)}) copy-start(f32[640]{0:T(1024)S(1)} %get-tuple-element.974) | copy-start | bytes 7684
  77.3 7.9 %copy-start = (f32[2,256,640]{2,1,0:T(8,128)S(1)}, f32[2,256,640]{2,1,0:T(8,128)}, u32[]{:S(2)}) copy-start(f32[2,256,640]{2,1,0:T(8,128)} %param.20) | copy-start | bytes 3932164
  105.4 71.7 %all-gather.15.cloned.1.call-start = ((), (), s32[]{:S(2)}) async-start(), calls=%async_computation.12 | async-start | bytes 2949120 | tf_op jit(solution)/shard_map/all_gather | solution.py:213
  107.6 104.4 %all-gather.13.cloned.1.call-start = ((), (), s32[]{:S(2)}) async-start(), calls=%async_computation.10 | async-start | bytes 2949120 | tf_op jit(solution)/shard_map/all_gather | solution.py:203
  108.2 138.2 %all-gather.17.cloned.1.call-start = ((), (), s32[]{:S(2)}) async-start(), calls=%async_computation.14 | async-start | bytes 2949120 | tf_op jit(solution)/shard_map/all_gather | solution.py:213
  108.8 178.3 %reduce-scatter.13.cloned.1.call-start = ((), (), s32[]{:S(2)}) async-start(), calls=%async_computation.13 | async-start | bytes 2949120 | tf_op jit(solution)/shard_map/reduce_scatter | solution.py:216
  177.1 10.1 %copy-start.51 = (bf16[2,640,640]{2,1,0:T(8,128)(2,1)S(1)}, bf16[2,640,640]{2,1,0:T(8,128)(2,1)}, u32[]{:S(2)}) copy-start(bf16[2,640,640]{2,1,0:T(8,128)(2,1)} %all-gather.11.cloned.1.call-done) | copy-start | bytes 4915204
  190.9 133.2 %reduce-scatter.15.cloned.1.call-start = ((), (), s32[]{:S(2)}) async-start(), calls=%async_computation.15 | async-start | bytes 2949120 | tf_op jit(solution)/shard_map/reduce_scatter | solution.py:216
  246.4 10.1 %copy-start.52 = (bf16[2,640,640]{2,1,0:T(8,128)(2,1)S(1)}, bf16[2,640,640]{2,1,0:T(8,128)(2,1)}, u32[]{:S(2)}) copy-start(bf16[2,640,640]{2,1,0:T(8,128)(2,1)} %all-gather.11.cloned.1.call-done) | copy-start | bytes 4915204
  260.3 102.9 %reduce-scatter.11.cloned.1.call-start = ((), (), s32[]{:S(2)}) async-start(), calls=%async_computation.11 | async-start | bytes 2949120 | tf_op jit(solution)/shard_map/reduce_scatter | solution.py:207
  266.4 135.7 %reduce-scatter.9.cloned.1.call-start = ((), (), s32[]{:S(2)}) async-start(), calls=%async_computation.9 | async-start | bytes 2949120 | tf_op jit(solution)/shard_map/reduce_scatter | solution.py:207
  272.8 205.9 %reduce-scatter.17.cloned.1.call-start = ((), (), s32[]{:S(2)}) async-start(), calls=%async_computation.16 | async-start | bytes 2048000 | tf_op jit(solution)/shard_map/reduce_scatter | solution.py:242
  285.4 116.8 %copy-start.13 = (f32[2,256,640]{2,1,0:T(8,128)S(1)}, f32[2,256,640]{2,1,0:T(8,128)}, u32[]{:S(2)}) copy-start(f32[2,256,640]{2,1,0:T(8,128)} %param.21) | copy-start | bytes 3932164
  286.9 335.1 %reduce-scatter.19.cloned.1.call-start = ((), (), s32[]{:S(2)}) async-start(), calls=%async_computation.17 | async-start | bytes 6758400
  407.4 18.9 %copy-start.26 = (s32[256]{0:T(256)S(1)}, s32[256]{0:T(256)}, u32[]{:S(2)}) copy-start(s32[256]{0:T(256)} %copy-done.25) | copy-start | bytes 3076
  426.3 31.9 %copy-start.12 = (bf16[256,640]{0,1:T(8,128)(2,1)S(1)}, bf16[256,640]{0,1:T(8,128)(2,1)}, u32[]{:S(2)}) copy-start(bf16[256,640]{0,1:T(8,128)(2,1)} %copy-done.11) | copy-start | bytes 983044
  426.3 32.4 %copy-start.3 = (f32[256,640]{1,0:T(8,128)S(1)}, f32[256,640]{1,0:T(8,128)}, u32[]{:S(2)}) copy-start(f32[256,640]{1,0:T(8,128)} %copy-done.2) | copy-start | bytes 1966084
  481.9 6.9 %copy-start.9 = (f32[2,160,640]{2,1,0:T(8,128)}, f32[2,160,640]{2,1,0:T(8,128)S(1)}, u32[]{:S(2)}) copy-start(f32[2,160,640]{2,1,0:T(8,128)S(1)} %get-tuple-element.915) | copy-start | bytes 2457604
  484.4 43.4 %copy-start.20 = (f32[1,256,640]{2,1,0:T(8,128)S(1)}, f32[1,256,640]{2,1,0:T(8,128)}, u32[]{:S(2)}) copy-start(f32[1,256,640]{2,1,0:T(8,128)} %get-tuple-element.966) | copy-start | bytes 1966084
  486.7 43.3 %copy-start.46 = (f32[256]{0:T(256)S(1)}, f32[256]{0:T(256)}, u32[]{:S(2)}) copy-start(f32[256]{0:T(256)} %copy-done.45) | copy-start | bytes 3076
  486.7 43.3 %copy-start.44 = (f32[256]{0:T(256)S(1)}, f32[256]{0:T(256)}, u32[]{:S(2)}) copy-start(f32[256]{0:T(256)} %copy-done.43) | copy-start | bytes 3076
  531.9 91.1 %copy-start.21 = (f32[640,80]{1,0:T(8,128)S(1)}, f32[640,80]{1,0:T(8,128)}, u32[]{:S(2)}) copy-start(f32[640,80]{1,0:T(8,128)} %copy.72) | copy-start | bytes 614404
  531.9 91.1 %copy-start.22 = (f32[640,80]{1,0:T(8,128)S(1)}, f32[640,80]{1,0:T(8,128)}, u32[]{:S(2)}) copy-start(f32[640,80]{1,0:T(8,128)} %copy.71) | copy-start | bytes 614404
  534.0 93.5 %copy-start.49 = (f32[80]{0:T(128)}, f32[80]{0:T(128)S(1)}, u32[]{:S(2)}) copy-start(f32[80]{0:T(128)S(1)} %get-tuple-element.919) | copy-start | bytes 964
  (35 other events, 85.4 us)
Sparse Core Ops, SparseCore 0:
  11.4 62.0 all-gather.6
  76.0 30.5 all-gather.10
  108.8 33.8 all-gather.8
  144.2 32.8 all-gather.14
  179.1 32.8 all-gather.12
  213.5 32.8 all-gather.16
  248.7 36.4 reduce-scatter.12
  287.6 36.4 reduce-scatter.14
  326.4 36.8 reduce-scatter.10
  365.4 36.6 reduce-scatter.8
  405.1 30.4 reduce-scatter.16
  475.2 146.7 reduce-scatter.18
where the time goes:
time: 642 us; the launch traced here: 635 us
  waiting for transfers between devices  305 us (48%)
  matrix products  128 us (20%)
  blocking collectives  81.1 us (13%)
  local copies, waits for them, and re-layouts  62.4 us (10%)
  other arithmetic  39.3 us (6%)
  between operations  15.3 us (2%)
    unnamed x13, waiting for transfers between devices  88.6 us
    unnamed x2, blocking collectives  81.1 us
    reduce_scatter x2, waiting for transfers between devices, local(): lax.psum_scatter(contract_cols(activ_low, ffn_rows[1]).astype(jnp.bfloat1...  75 us
    dot_general x8, matrix products, matmul(): return jnp.dot(left_side, right_side, preferred_element_type=jnp.float32)  61.2 us
    all_gather x2, waiting for transfers between devices, local(): normed_all = lax.all_gather(normed_two_low, 'col', axis=0, tiled=True)  54.5 us
    reduce_scatter x2, waiting for transfers between devices, local(): lax.psum_scatter(contract_cols(grad_up, ffn_rows[0]).astype(jnp.bfloat16)...  35.8 us
    all_gather x2, waiting for transfers between devices, local(): grad_all = lax.all_gather(grad_out_low, 'col', axis=0, tiled=True)  35.7 us
    dot_general x8, matrix products, contract_cols(): lax.dot_general(left_side, right_side, (((1,), (1,)), ((), ())), preferre...  28 us
  transfers between devices with their start and end apart: 12, of which 9 were waited for; matrix products, arithmetic and copies ran while one was open for 34% of the time, Pallas kernels for 0%

commit v1 on v0

--- a/solution.py
+++ b/solution.py
@@ -13,6 +13,16 @@
 AVERAGE_DECAY = 0.85
 RATE_SCALE = 0.06
 MASKED = -1e30
+
+
+def gather_around(x, axis, dim):
+    ways, here, lap = (lax.axis_size(axis), lax.axis_index(axis), x.shape[dim])
+    shape = [n * ways if d == dim else n for d, n in enumerate(x.shape)]
+    full = lax.dynamic_update_slice_in_dim(jnp.zeros(shape, x.dtype), x, here * lap, axis=dim)
+    for far in range(1, ways):
+        x = lax.ppermute(x, axis, [(d, (d + 1) % ways) for d in range(ways)])
+        full = lax.dynamic_update_slice_in_dim(full, x, (here - far) % ways * lap, axis=dim)
+    return full
 
 
 def layer_norm(values, gain, shift):
@@ -210,7 +220,7 @@
             scatter_dimension=0,
             tiled=True,
         ).astype(jnp.float32)
-        grad_all = lax.all_gather(grad_out_low, "col", axis=0, tiled=True)
+        grad_all = gather_around(grad_out_low, "col", 0)
         grad_act = matmul(grad_all, ffn_rows[1])
         grad_up = pull_gelu(grad_act)[0].astype(jnp.bfloat16)
         grad_normed_two = lax.psum_scatter(

time: 642 us -> 616 us (0.960)
  waiting for transfers between devices: 305 us -> 264 us
  local copies, waits for them, and re-layouts: 62.4 us -> 82.3 us
  matrix products: 128 us -> 121 us
    ppermute x0 -> x14, waiting for transfers between devices: none -> 60.8 us  [gather_around(): x = lax.ppermute(x, axis, [(d, (d + 1) % ways) for d in range(ways)])]
    all_gather x2, waiting for transfers between devices: 54.5 us -> 2.65 us  [local(): normed_all = lax.all_gather(normed_two_low, 'col', axis=0, tiled=True)]
    all_gather x2 -> x0, waiting for transfers between devices: 35.7 us -> none  [local(): grad_all = lax.all_gather(grad_out_low, 'col', axis=0, tiled=True)]
    dynamic_update_slice x0 -> x16, local copies, waits for them, and re-layouts: none -> 19.1 us  [the longest x14 16.5 us: gather_around(): lax.dynamic_update_slice_in_dim(full, x, (here - far) % ways * lap, axis=...]
    reduce_scatter x2, waiting for transfers between devices: 35.8 us -> 22.2 us  [local(): lax.psum_scatter(contract_cols(grad_up, ffn_rows[0]).astype(jnp.bfloat16)...]
    dot_general x8, matrix products: 61.2 us -> 51.9 us  [matmul(): return jnp.dot(left_side, right_side, preferred_element_type=jnp.float32)]
    unnamed x13 -> x11, waiting for transfers between devices: 88.6 us -> 87.9 us
    unnamed x123 -> x131, local copies, waits for them, and re-layouts: 25.9 us -> 25.5 us
  transfers between devices with their start and end apart: 12 -> 24, of which waited for: 9 -> 19; matrix products, arithmetic and copies ran while one was open for 34% -> 38% of each run, Pallas kernels for 0% -> 0%
where the time goes in v1:
time: 616 us; the launch traced here: 607 us
  waiting for transfers between devices  264 us (43%)
  matrix products  121 us (20%)
  local copies, waits for them, and re-layouts  82.3 us (13%)
  blocking collectives  81.2 us (13%)
  other arithmetic  39.3 us (6%)
  between operations  15.4 us (2%)
    unnamed x11, waiting for transfers between devices  87.9 us
    unnamed x2, blocking collectives  81.2 us
    reduce_scatter x2, waiting for transfers between devices, local(): lax.psum_scatter(contract_cols(activ_low, ffn_rows[1]).astype(jnp.bfloat1...  74.7 us
    ppermute x14, waiting for transfers between devices, gather_around(): x = lax.ppermute(x, axis, [(d, (d + 1) % ways) for d in range(ways)])  60.8 us
    dot_general x8, matrix products, matmul(): return jnp.dot(left_side, right_side, preferred_element_type=jnp.float32)  51.9 us
    dot_general x8, matrix products, contract_cols(): lax.dot_general(left_side, right_side, (((1,), (1,)), ((), ())), preferre...  28.1 us
    unnamed x131, local copies, waits for them, and re-layouts  25.5 us
    reduce_scatter x2, waiting for transfers between devices, local(): lax.psum_scatter(contract_cols(grad_up, ffn_rows[0]).astype(jnp.bfloat16)...  22.2 us
  transfers between devices with their start and end apart: 24, of which 19 were waited for; matrix products, arithmetic and copies ran while one was open for 38% of the time, Pallas kernels for 0%

profile of v1, /device:TPU:0, one launch (start us, length us, event | category | flops | bytes accessed | tf_op | source)
XLA Modules:
  0.0 606.8 jit_solution(3737295837318982431)
XLA Ops:
  15.9 42.1 %all-reduce = bf16[2560]{0:T(1024)(128)(2,1)S(1)} all-reduce(bf16[2560]{0:T(1024)(128)(2,1)S(1)} %dynamic-update-slice), channel_id=1, replica_groups=mesh['row'=4,'col'=8] {'row','col'}, use_global_device_ids=true, to_apply=%add | all-reduce | flops 2560 | bytes 10240
  58.1 15.5 %all-gather.5.cloned.1.call-done = bf16[640,2560]{0,1:T(8,128)(2,1)} async-done(((bf16[640,80]{0,1:T(8,128)(2,1)}), bf16[640,2560]{0,1:T(8,128)(2,1)}) %all-gather.5.cloned.1.call-update) | async-done | bytes 3276816 | tf_op jit(solution)/shard_map/all_gather | solution.py:181
  77.3 5.3 while.73
  85.1 4.0 convolution_convert_fusion.5
  91.5 8.2 %while.72 = (s32[]{:T(128)}, bf16[256,640]{0,1:T(8,128)(2,1)}, f32[20,256]{1,0:T(8,128)S(1)}, f32[20,256]{1,0:T(8,128)S(1)}, bf16[256,1920]{0,1:T(8,128)(2,1)S(1...) while((s32[]{:T(128)}, bf16[256,640]{0,1:T(8,128)(2,1)}, ...), condition=%wide.region_5.6_spmd.clone, body=%wide.region_2.5_spmd.clone.sunk | while | flops 35715084 | bytes 4101494 | solution.py:109
  112.3 5.0 collective-permute-done
  117.3 3.7 collective-permute-done.7
  121.0 11.4 %collective-permute-done.1 = bf16[256,640]{1,0:T(8,128)(2,1)S(1)} collective-permute-done((bf16[256,640]{1,0:T(8,128)(2,1)S(1)}, bf16[256,640]{1,0:T(8,128)(2,1)S(1)}, u32[]{:S(2)}, u32[]{:S(2)}) %collective-permute-start.1) | collective-permute-done | bytes 327712 | tf_op jit(solution)/shard_map/ppermute | solution.py:23
  132.3 10.6 %collective-permute-done.8 = bf16[256,640]{1,0:T(8,128)(2,1)} collective-permute-done((bf16[256,640]{1,0:T(8,128)(2,1)S(1)}, bf16[256,640]{1,0:T(8,128)(2,1)}, u32[]{:S(2)}, u32[]{:S(2)}) %collective-permute-start.8) | collective-permute-done | bytes 327712 | tf_op jit(solution)/shard_map/ppermute | solution.py:23
  143.0 9.6 %collective-permute-done.2 = bf16[256,640]{1,0:T(8,128)(2,1)S(1)} collective-permute-done((bf16[256,640]{1,0:T(8,128)(2,1)S(1)}, bf16[256,640]{1,0:T(8,128)(2,1)S(1)}, u32[]{:S(2)}, u32[]{:S(2)}) %collective-permute-start.2) | collective-permute-done | bytes 327712 | tf_op jit(solution)/shard_map/ppermute | solution.py:23
  152.8 3.4 collective-permute-done.9
  173.8 3.7 collective-permute-done.5
  182.2 3.7 collective-permute-done.6
  186.9 15.0 %multiply_convert_fusion.3 = (bf16[2048,640]{1,0:T(8,128)(2,1)}, f32[2048,640]{1,0:T(8,128)S(1)}, f32[2048,640]{1,0:T(8,128)S(1)}) fusion(bf16[2048,640]{1,0:T(8,128)(2,1)} %all-gather.7.cloned.1.call-done, bf16[2,640,640]{2,1,0:T(8,128)(2,1)} %all-gather.9.cloned.1.call-done), kind=kOutput, calls=%fused_computation.92 | convolution fusion | flops 1762918400 | bytes 16547840 | tf_op jit(solution)/shard_map/dot_general | solution.py:39
  201.9 5.5 add_convert_fusion.1
  208.9 3.8 convolution_convert_fusion.1
  218.8 15.0 %multiply_convert_fusion.2 = (bf16[2048,640]{1,0:T(8,128)(2,1)}, f32[2048,640]{1,0:T(8,128)S(1)}, f32[2048,640]{1,0:T(8,128)S(1)}) fusion(bf16[2048,640]{1,0:T(8,128)(2,1)} %all-gather.11.cloned.1.call-done, bf16[2,640,640]{2,1,0:T(8,128)(2,1)} %all-gather.9.cloned.1.call-done), kind=kOutput, calls=%fused_computation.79 | convolution fusion | flops 1762918400 | bytes 16547840 | tf_op jit(solution)/shard_map/dot_general | solution.py:39
  233.8 5.4 add_convert_fusion
  240.8 3.8 convolution_convert_fusion
  244.6 6.0 convolution_convert_fusion.2
  251.1 6.0 convolution_convert_fusion.3
  257.2 4.9 convolution_bitcast_fusion
  262.2 4.2 convolution_bitcast_fusion.2
  274.0 22.2 %reduce-scatter.15.cloned.1.call-done = bf16[256,640]{1,0:T(8,128)(2,1)} async-done(((bf16[2048,640]{1,0:T(8,128)(2,1)}), bf16[256,640]{1,0:T(8,128)(2,1)}) %reduce-scatter.15.cloned.1.call-update) | async-done | bytes 327696 | tf_op jit(solution)/shard_map/reduce_scatter | solution.py:226
  299.2 35.8 %reduce-scatter.11.cloned.1.call-done = bf16[256,640]{1,0:T(8,128)(2,1)} async-done(((bf16[2048,640]{1,0:T(8,128)(2,1)}), bf16[256,640]{1,0:T(8,128)(2,1)}) %reduce-scatter.11.cloned.1.call-update) | async-done | bytes 327696 | tf_op jit(solution)/shard_map/reduce_scatter | solution.py:217
  335.0 38.9 %reduce-scatter.9.cloned.1.call-done = bf16[256,640]{1,0:T(8,128)(2,1)} async-done(((bf16[2048,640]{1,0:T(8,128)(2,1)}), bf16[256,640]{1,0:T(8,128)(2,1)}) %reduce-scatter.9.cloned.1.call-update) | async-done | bytes 327696 | tf_op jit(solution)/shard_map/reduce_scatter | solution.py:217
  379.2 15.2 %while.74 = (s32[]{:T(128)}, bf16[256,1920]{0,1:T(8,128)(2,1)S(1)}, bf16[256,1920]{0,1:T(8,128)(2,1)}, f32[20,256]{1,0:T(8,128)S(1)}, f32[20,256]{1,0:T(8,128)S(...) while((s32[]{:T(128)}, bf16[256,1920]{0,1:T(8,128)(2,1)S(1)}, ...), condition=%wide.region_23.24_spmd.clone, body=%wide.region_21.23_spmd.clone.sunk | while | flops 86703120 | bytes 9733514 | solution.py:156
  398.1 32.0 %while.75 = (s32[]{:T(128)}, bf16[256,1920]{0,1:T(8,128)(2,1)}, bf16[256,1920]{0,1:T(8,128)(2,1)}, f32[20,256]{1,0:T(8,128)}, f32[20,256]{1,0:T(8,128)}, /*index...) while((s32[]{:T(128)}, bf16[256,1920]{0,1:T(8,128)(2,1)}, ...), condition=%wide.region_31.32_spmd.clone, body=%wide.region_29.31_spmd.clone.sunk | while | flops 86703120 | bytes 9733514 | solution.py:156
  435.4 3.3 maximum_add_fusion
  438.7 8.2 %copy.87 = f32[640,2560]{0,1:T(8,128)} copy(f32[640,2560]{1,0:T(8,128)} %maximum_add_fusion) | data formatting | bytes 13107200
  460.6 39.1 %all-reduce.1 = f32[2560]{0:T(1024)S(1)} all-reduce(f32[2560]{0:T(1024)S(1)} %maximum_add_fusion.2), channel_id=7, replica_groups=mesh['row'=4,'col'=8] {'row','col'}, use_global_device_ids=true, to_apply=%region_43.44.clone | all-reduce | flops 2560 | bytes 20480
  506.4 87.8 %reduce-scatter.19.cloned.1.call-done = f32[80,640]{1,0:T(8,128)} async-done(((f32[2560,640]{1,0:T(8,128)}), f32[80,640]{1,0:T(8,128)}) %reduce-scatter.19.cloned.1.call-update) | async-done | bytes 204816
  (466 shorter events, 172.5 us)
Async XLA Ops:
  7.2 66.4 %all-gather.5.cloned.1.call-start = ((), (), s32[]{:S(2)}) async-start(), calls=%async_computation.6 | async-start | bytes 3379200 | tf_op jit(solution)/shard_map/all_gather | solution.py:181
  8.8 178.0 %all-gather.9.cloned.1.call-start = ((), (), s32[]{:S(2)}) async-start(), calls=%async_computation.8 | async-start | bytes 2048000 | tf_op jit(solution)/shard_map/all_gather | solution.py:191
  10.9 176.0 %all-gather.7.cloned.1.call-start = ((), (), s32[]{:S(2)}) async-start(), calls=%async_computation.7 | async-start | bytes 2949120 | tf_op jit(solution)/shard_map/all_gather | solution.py:213
  13.8 63.5 %copy-start.41 = (f32[256]{0:T(256)}, f32[256]{0:T(256)S(1)}, u32[]{:S(2)}) copy-start(f32[256]{0:T(256)S(1)} %get-tuple-element.986) | copy-start | bytes 3076
  13.8 68.8 %copy-start.43 = (f32[256]{0:T(256)}, f32[256]{0:T(256)S(1)}, u32[]{:S(2)}) copy-start(f32[256]{0:T(256)S(1)} %get-tuple-element.987) | copy-start | bytes 3076
  15.4 67.2 %copy-start.45 = (f32[256]{0:T(256)}, f32[256]{0:T(256)S(1)}, u32[]{:S(2)}) copy-start(f32[256]{0:T(256)S(1)} %fusion.77) | copy-start | bytes 3076
  15.4 61.8 %copy-start.47 = (f32[256]{0:T(256)}, f32[256]{0:T(256)S(1)}, u32[]{:S(2)}) copy-start(f32[256]{0:T(256)S(1)} %fusion.79) | copy-start | bytes 3076
  105.4 113.5 %all-gather.11.cloned.1.call-start = ((), (), s32[]{:S(2)}) async-start(), calls=%async_computation.10 | async-start | bytes 2949120 | tf_op jit(solution)/shard_map/all_gather | solution.py:213
  109.0 8.3 %collective-permute-start = (bf16[256,640]{1,0:T(8,128)(2,1)S(1)}, bf16[256,640]{1,0:T(8,128)(2,1)S(1)}, u32[]{:S(2)}, u32[]{:S(2)}) collective-permute-start(bf16[256,640]{1,0:T(8,128)(2,1)S(1)} %get-tuple-element.929), channel_id=1, source_target_pairs={{0,1},{1,2},{2,3},{3,4},{4,5},{5,6},{6,7},{7,0},{8,9},{9,10},{10,1... | collective-permute-start | bytes 983048 | tf_op jit(solution)/shard_map/ppermute | solution.py:23
  111.7 9.3 %collective-permute-start.7 = (bf16[256,640]{1,0:T(8,128)(2,1)S(1)}, bf16[256,640]{1,0:T(8,128)(2,1)S(1)}, u32[]{:S(2)}, u32[]{:S(2)}) collective-permute-start(bf16[256,640]{1,0:T(8,128)(2,1)S(1)} %get-tuple-element.931), channel_id=1, source_target_pairs={{0,1},{1,2},{2,3},{3,4},{4,5},{5,6},{6,7},{7,0},{8,9},{9,10},{10,1... | collective-permute-start | bytes 983048 | tf_op jit(solution)/shard_map/ppermute | solution.py:23
  117.3 15.0 %collective-permute-start.1 = (bf16[256,640]{1,0:T(8,128)(2,1)S(1)}, bf16[256,640]{1,0:T(8,128)(2,1)S(1)}, u32[]{:S(2)}, u32[]{:S(2)}) collective-permute-start(bf16[256,640]{1,0:T(8,128)(2,1)S(1)} %collective-permute-done), channel_id=1, source_target_pairs={{0,1},{1,2},{2,3},{3,4},{4,5},{5,6},{6,7},{7,0},{8,9},{9,10},{10,1... | collective-permute-start | bytes 983048 | tf_op jit(solution)/shard_map/ppermute | solution.py:23
  120.9 22.0 %collective-permute-start.8 = (bf16[256,640]{1,0:T(8,128)(2,1)S(1)}, bf16[256,640]{1,0:T(8,128)(2,1)}, u32[]{:S(2)}, u32[]{:S(2)}) collective-permute-start(bf16[256,640]{1,0:T(8,128)(2,1)S(1)} %collective-permute-done.7), channel_id=1, source_target_pairs={{0,1},{1,2},{2,3},{3,4},{4,5},{5,6},{6,7},{7,0},{8,9},{9,10},{10,1... | collective-permute-start | bytes 983048 | tf_op jit(solution)/shard_map/ppermute | solution.py:23
  132.3 20.3 %collective-permute-start.2 = (bf16[256,640]{1,0:T(8,128)(2,1)S(1)}, bf16[256,640]{1,0:T(8,128)(2,1)S(1)}, u32[]{:S(2)}, u32[]{:S(2)}) collective-permute-start(bf16[256,640]{1,0:T(8,128)(2,1)S(1)} %collective-permute-done.1), channel_id=1, source_target_pairs={{0,1},{1,2},{2,3},{3,4},{4,5},{5,6},{6,7},{7,0},{8,9},{9,10},{10,1... | collective-permute-start | bytes 983048 | tf_op jit(solution)/shard_map/ppermute | solution.py:23
  142.9 13.3 %collective-permute-start.9 = (bf16[256,640]{1,0:T(8,128)(2,1)}, bf16[256,640]{1,0:T(8,128)(2,1)}, u32[]{:S(2)}, u32[]{:S(2)}) collective-permute-start(bf16[256,640]{1,0:T(8,128)(2,1)} %collective-permute-done.8), channel_id=1, source_target_pairs={{0,1},{1,2},{2,3},{3,4},{4,5},{5,6},{6,7},{7,0},{8,9},{9,10},{10,1... | collective-permute-start | bytes 983048 | tf_op jit(solution)/shard_map/ppermute | solution.py:23
  152.6 8.3 %collective-permute-start.3 = (bf16[256,640]{1,0:T(8,128)(2,1)S(1)}, bf16[256,640]{1,0:T(8,128)(2,1)S(1)}, u32[]{:S(2)}, u32[]{:S(2)}) collective-permute-start(bf16[256,640]{1,0:T(8,128)(2,1)S(1)} %collective-permute-done.2), channel_id=1, source_target_pairs={{0,1},{1,2},{2,3},{3,4},{4,5},{5,6},{6,7},{7,0},{8,9},{9,10},{10,1... | collective-permute-start | bytes 983048 | tf_op jit(solution)/shard_map/ppermute | solution.py:23
  156.2 8.5 %collective-permute-start.10 = (bf16[256,640]{1,0:T(8,128)(2,1)}, bf16[256,640]{1,0:T(8,128)(2,1)S(1)}, u32[]{:S(2)}, u32[]{:S(2)}) collective-permute-start(bf16[256,640]{1,0:T(8,128)(2,1)} %collective-permute-done.9), channel_id=1, source_target_pairs={{0,1},{1,2},{2,3},{3,4},{4,5},{5,6},{6,7},{7,0},{8,9},{9,10},{10,1... | collective-permute-start | bytes 983048 | tf_op jit(solution)/shard_map/ppermute | solution.py:23
  161.0 8.3 %collective-permute-start.4 = (bf16[256,640]{1,0:T(8,128)(2,1)S(1)}, bf16[256,640]{1,0:T(8,128)(2,1)S(1)}, u32[]{:S(2)}, u32[]{:S(2)}) collective-permute-start(bf16[256,640]{1,0:T(8,128)(2,1)S(1)} %collective-permute-done.3), channel_id=1, source_target_pairs={{0,1},{1,2},{2,3},{3,4},{4,5},{5,6},{6,7},{7,0},{8,9},{9,10},{10,1... | collective-permute-start | bytes 983048 | tf_op jit(solution)/shard_map/ppermute | solution.py:23
  164.7 8.3 %collective-permute-start.11 = (bf16[256,640]{1,0:T(8,128)(2,1)S(1)}, bf16[256,640]{1,0:T(8,128)(2,1)S(1)}, u32[]{:S(2)}, u32[]{:S(2)}) collective-permute-start(bf16[256,640]{1,0:T(8,128)(2,1)S(1)} %collective-permute-done.10), channel_id=1, source_target_pairs={{0,1},{1,2},{2,3},{3,4},{4,5},{5,6},{6,7},{7,0},{8,9},{9,10},{10,1... | collective-permute-start | bytes 983048 | tf_op jit(solution)/shard_map/ppermute | solution.py:23
  169.3 8.3 %collective-permute-start.5 = (bf16[256,640]{1,0:T(8,128)(2,1)S(1)}, bf16[256,640]{1,0:T(8,128)(2,1)S(1)}, u32[]{:S(2)}, u32[]{:S(2)}) collective-permute-start(bf16[256,640]{1,0:T(8,128)(2,1)S(1)} %collective-permute-done.4), channel_id=1, source_target_pairs={{0,1},{1,2},{2,3},{3,4},{4,5},{5,6},{6,7},{7,0},{8,9},{9,10},{10,1... | collective-permute-start | bytes 983048 | tf_op jit(solution)/shard_map/ppermute | solution.py:23
  173.0 8.4 %collective-permute-start.12 = (bf16[256,640]{1,0:T(8,128)(2,1)S(1)}, bf16[256,640]{1,0:T(8,128)(2,1)}, u32[]{:S(2)}, u32[]{:S(2)}) collective-permute-start(bf16[256,640]{1,0:T(8,128)(2,1)S(1)} %collective-permute-done.11), channel_id=1, source_target_pairs={{0,1},{1,2},{2,3},{3,4},{4,5},{5,6},{6,7},{7,0},{8,9},{9,10},{10,1... | collective-permute-start | bytes 983048 | tf_op jit(solution)/shard_map/ppermute | solution.py:23
  177.6 8.3 %collective-permute-start.6 = (bf16[256,640]{1,0:T(8,128)(2,1)S(1)}, bf16[256,640]{1,0:T(8,128)(2,1)S(1)}, u32[]{:S(2)}, u32[]{:S(2)}) collective-permute-start(bf16[256,640]{1,0:T(8,128)(2,1)S(1)} %collective-permute-done.5), channel_id=1, source_target_pairs={{0,1},{1,2},{2,3},{3,4},{4,5},{5,6},{6,7},{7,0},{8,9},{9,10},{10,1... | collective-permute-start | bytes 983048 | tf_op jit(solution)/shard_map/ppermute | solution.py:23
  181.4 34.0 %collective-permute-start.13 = (bf16[256,640]{1,0:T(8,128)(2,1)}, bf16[256,640]{1,0:T(8,128)(2,1)S(1)}, u32[]{:S(2)}, u32[]{:S(2)}) collective-permute-start(bf16[256,640]{1,0:T(8,128)(2,1)} %collective-permute-done.12), channel_id=1, source_target_pairs={{0,1},{1,2},{2,3},{3,4},{4,5},{5,6},{6,7},{7,0},{8,9},{9,10},{10,1... | collective-permute-start | bytes 983048 | tf_op jit(solution)/shard_map/ppermute | solution.py:23
  186.6 86.2 %reduce-scatter.13.cloned.1.call-start = ((), (), s32[]{:S(2)}) async-start(), calls=%async_computation.12 | async-start | bytes 2949120 | tf_op jit(solution)/shard_map/reduce_scatter | solution.py:226
  212.7 83.5 %reduce-scatter.15.cloned.1.call-start = ((), (), s32[]{:S(2)}) async-start(), calls=%async_computation.13 | async-start | bytes 2949120 | tf_op jit(solution)/shard_map/reduce_scatter | solution.py:226
  244.6 90.4 %reduce-scatter.11.cloned.1.call-start = ((), (), s32[]{:S(2)}) async-start(), calls=%async_computation.11 | async-start | bytes 2949120 | tf_op jit(solution)/shard_map/reduce_scatter | solution.py:217
  250.6 123.2 %reduce-scatter.9.cloned.1.call-start = ((), (), s32[]{:S(2)}) async-start(), calls=%async_computation.9 | async-start | bytes 2949120 | tf_op jit(solution)/shard_map/reduce_scatter | solution.py:217
  257.1 193.4 %reduce-scatter.17.cloned.1.call-start = ((), (), s32[]{:S(2)}) async-start(), calls=%async_computation.14 | async-start | bytes 2048000 | tf_op jit(solution)/shard_map/reduce_scatter | solution.py:252
  272.6 321.7 %reduce-scatter.19.cloned.1.call-start = ((), (), s32[]{:S(2)}) async-start(), calls=%async_computation.15 | async-start | bytes 6758400
  456.2 43.5 %copy-start.21 = (f32[1,256,640]{2,1,0:T(8,128)S(1)}, f32[1,256,640]{2,1,0:T(8,128)}, u32[]{:S(2)}) copy-start(f32[1,256,640]{2,1,0:T(8,128)} %get-tuple-element.968) | copy-start | bytes 1966084
  503.8 91.5 %copy-start.22 = (f32[640,80]{1,0:T(8,128)S(1)}, f32[640,80]{1,0:T(8,128)}, u32[]{:S(2)}) copy-start(f32[640,80]{1,0:T(8,128)} %copy.70) | copy-start | bytes 614404
  503.8 91.5 %copy-start.23 = (f32[640,80]{1,0:T(8,128)S(1)}, f32[640,80]{1,0:T(8,128)}, u32[]{:S(2)}) copy-start(f32[640,80]{1,0:T(8,128)} %copy.69) | copy-start | bytes 614404
  505.9 93.8 %copy-start.55 = (f32[80]{0:T(128)}, f32[80]{0:T(128)S(1)}, u32[]{:S(2)}) copy-start(f32[80]{0:T(128)S(1)} %get-tuple-element.919) | copy-start | bytes 964
  (51 other events, 465.0 us)
Sparse Core Ops, SparseCore 0:
  11.4 62.0 all-gather.4
  76.0 30.5 all-gather.8
  108.8 44.7 all-gather.6
  186.8 32.0 all-gather.10
  221.0 36.4 reduce-scatter.12
  259.7 36.4 reduce-scatter.14
  298.5 36.4 reduce-scatter.10
  337.3 36.5 reduce-scatter.8
  376.9 30.6 reduce-scatter.16
  447.0 147.1 reduce-scatter.18
